TPU v7x, 256 devices: a whole 4x4x8 slice. The times are simulated.
256 devices in a mesh: section: 2 (over y_hi), seq: 32 (over x, z), chan: 4 (over y_lo, core).
Axes of the slice: x: 4, y: 4 (y_hi: 2, y_lo: 2; y = y_hi * 2 + y_lo), z: 8, core: 2. Of those that a mesh axis runs over, the one named last changes fastest.
Arguments:
- bases: int32 [2, 2097152], P('section', 'seq'), may hold values from 0 to 3
- stem_embedding_weight: bfloat16 [512, 1536], P(None, 'chan'), may hold values from -1.64443437 to 1.64443437
- gains: float32 [3, 1536], replicated, may hold values from 0.1 to 1.9
- conv_weight: bfloat16 [3, 3, 1536, 1536], P(None, None, None, 'chan'), may hold values from -0.09375 to 0.09375
- dec_weight: bfloat16 [1536, 384], P('chan'), may hold values from -0.3125 to 0.3125
- upstream: bfloat16 [2, 16384, 1536], P('section', 'seq', 'chan'), may hold values from -0.032958984 to 0.032958984
Outputs:
- decoded: bfloat16 [2, 16384, 1536], P('section', 'seq', 'chan')
- weight_grad: float32 [1536, 384], P('chan')
All inputs are finite; a program needn't handle non-finite values.
Results may differ from a plain program's by a relative error of at most 0.0076.
Values may be sent and summed in bfloat16 or wider, within the bound.
No kernel may reach another device: no remote copies, remote signals or barrier semaphores. Data moves between devices by JAX's collectives and lax.ppermute only.
A program may use at most 128 MiB of HBM per device.

v0:
```python
import jax
import jax.numpy as jnp
from jax import lax
from jax.sharding import PartitionSpec as P

PATCH = 128
FIRST_DILATION0 = 2
EPSILON = 1e-06


def with_halo(shard, sides, width):
    for axis, dim in sides:
        size, length = (lax.axis_size(axis), shard.shape[dim])
        up = [(i, (i + 1) % size) for i in range(size - 1)]
        down = [(j, i) for i, j in up]
        last = lax.slice_in_dim(shard, length - width, length, axis=dim)
        initial = lax.slice_in_dim(shard, 0, width, axis=dim)
        before = lax.ppermute(last, axis, up)
        after = lax.ppermute(initial, axis, down)
        shard = jnp.concatenate([before, shard, after], axis=dim)
    return shard


def activate(rows, gain_row):
    widened = rows.astype(jnp.float32)
    inverse_rms = lax.rsqrt(jnp.mean(widened * widened, axis=-1, keepdims=True) + EPSILON)
    return jax.nn.gelu(widened * inverse_rms * gain_row).astype(jnp.bfloat16)


def apply_convolution(padded, kernel_taps, dilation_step, row_count):
    update = jnp.dot(padded[0:row_count], kernel_taps[0], preferred_element_type=jnp.float32)
    for offset in range(1, kernel_taps.shape[0]):
        start = offset * dilation_step
        update = update + jnp.dot(
            padded[start : start + row_count],
            kernel_taps[offset],
            preferred_element_type=jnp.float32,
        )
    return update


def body(bases, stem_embedding_weight, gains, conv_weight, dec_weight, upstream):
    row_count = upstream.shape[1]
    letters = bases.reshape(row_count, PATCH)
    onehot = letters[:, :, None] == jnp.arange(4, dtype=jnp.int32)[None, None, :]
    onehot = onehot.astype(jnp.bfloat16).reshape(row_count, PATCH * 4)
    stream = jnp.dot(onehot, stem_embedding_weight, preferred_element_type=jnp.float32).astype(
        jnp.bfloat16
    )
    for tower_layer_index in range(conv_weight.shape[0]):
        dilation_step = FIRST_DILATION0 * 2**tower_layer_index
        full_rows = lax.all_gather(stream, "chan", axis=1, tiled=True)
        padded = with_halo(
            activate(full_rows, gains[tower_layer_index]), (("seq", 0),), dilation_step
        )
        update = apply_convolution(padded, conv_weight[tower_layer_index], dilation_step, row_count)
        stream = (stream.astype(jnp.float32) + update).astype(jnp.bfloat16)
    decoded = jnp.dot(stream, dec_weight, preferred_element_type=jnp.float32).astype(jnp.bfloat16)
    upstream_rows = upstream[0]
    contract_row_pairs = (((0,), (0,)), ((), ()))
    partial_grad = lax.dot_general(
        stream, upstream_rows, contract_row_pairs, preferred_element_type=jnp.float32
    )
    weight_grad = lax.psum(partial_grad, ("section", "seq"))
    return (decoded[None], weight_grad)


def solution(mesh):
    placed = (
        P("section", "seq"),
        P(None, "chan"),
        P(),
        P(None, None, None, "chan"),
        P("chan", None),
        P("section", "seq", "chan"),
    )
    return jax.shard_map(
        body,
        mesh=mesh,
        in_specs=placed,
        out_specs=(P("section", "seq", "chan"), P("chan", None)),
        check_vma=False,
    )
```

profile of v0, /device:TPU:24, one launch (start us, length us, event | category | flops | bytes accessed | tf_op | source)
XLA Modules:
  0.0 813.8 jit_solution(4729358638135030658)
XLA Ops:
  7.2 0.0 copy-start
  7.2 0.0 all-gather.4.cloned.1.call-start
  7.2 0.1 eq.26
  7.4 1.1 copy.8
  8.4 0.2 eq.23
  8.6 0.4 eq.24
  9.0 1.3 convolution_convert_fusion.1
  10.3 0.0 all-gather.4.cloned.1.call-update
  10.4 0.0 all-gather.6.cloned.1.call-start
  10.4 0.1 slice_reduce_fusion
  10.5 29.4 %all-gather.4.cloned.1.call-done = bf16[512,1536]{1,0:T(8,128)(2,1)} async-done(((bf16[512,384]{1,0:T(8,128)(2,1)}), bf16[512,1536]{1,0:T(8,128)(2,1)}) %all-gather.4.cloned.1.call-update) | async-done | bytes 1572880 | tf_op jit(solution)/shard_map/all_gather | solution.py:52
  39.8 1.8 fusion
  41.6 2.8 fusion.4
  44.5 3.5 collective-permute-start
  47.9 1.3 collective-permute-start.1
  49.2 2.2 fusion.60
  51.5 0.0 copy-start.1
  51.5 2.0 collective-permute-done.1
  53.4 2.3 fusion.38
  55.7 3.1 fusion.49
  58.8 0.0 all-gather.6.cloned.1.call-update
  58.8 0.0 all-gather.8.cloned.1.call-start
  58.8 28.8 %all-gather.6.cloned.1.call-done = bf16[512,1536]{1,0:T(8,128)(2,1)} async-done(((bf16[512,384]{1,0:T(8,128)(2,1)}), bf16[512,1536]{1,0:T(8,128)(2,1)}) %all-gather.6.cloned.1.call-update) | async-done | bytes 1572880 | tf_op jit(solution)/shard_map/all_gather | solution.py:52
  87.6 1.8 fusion.9
  89.4 2.8 fusion.13
  92.2 1.3 collective-permute-start.3
  93.5 2.2 fusion.56
  95.8 0.0 copy-start.3
  95.8 4.7 collective-permute-start.2
  100.5 2.3 fusion.34
  102.8 3.0 add_convert_fusion.1
  105.8 0.0 all-gather.8.cloned.1.call-update
  105.9 0.0 all-reduce.2.cloned.1.call-start
  105.9 29.4 %all-gather.8.cloned.1.call-done = bf16[512,1536]{1,0:T(8,128)(2,1)} async-done(((bf16[512,384]{1,0:T(8,128)(2,1)}), bf16[512,1536]{1,0:T(8,128)(2,1)}) %all-gather.8.cloned.1.call-update) | async-done | bytes 1572880 | tf_op jit(solution)/shard_map/all_gather | solution.py:52
  135.3 1.8 fusion.18
  137.1 2.8 fusion.22
  139.9 1.5 collective-permute-start.5
  141.4 2.2 fusion.52
  143.7 0.0 copy-start.2
  143.7 4.7 collective-permute-start.4
  148.4 2.2 fusion.30
  150.6 0.0 copy-start.5
  150.7 2.3 add_convert_fusion
  153.0 1.2 fusion.74
  154.3 0.0 all-reduce.2.cloned.1.call-update
  154.3 1.1 fusion.50
  155.4 649.9 %all-reduce.2.cloned.1.call-done = f32[384,384]{1,0:T(8,128)} async-done(((f32[384,384]{1,0:T(8,128)}), f32[384,384]{1,0:T(8,128)}) %all-reduce.2.cloned.1.call-update) | async-done | bytes 589840 | tf_op jit(solution)/shard_map/psum | solution.py:64
  805.3 1.9 copy.10
  (21 shorter events, 0.1 us)
Async XLA Ops:
  7.2 1.8 copy-start
  7.2 3.2 copy-start.6
  7.2 32.7 %all-gather.4.cloned.1.call-start = ((), (), s32[]{:S(2)}) async-start(), calls=%async_computation | async-start | bytes 1966080 | tf_op jit(solution)/shard_map/all_gather | solution.py:52
  10.4 77.3 %all-gather.6.cloned.1.call-start = ((), (), s32[]{:S(2)}) async-start(), calls=%async_computation.1 | async-start | bytes 1966080 | tf_op jit(solution)/shard_map/all_gather | solution.py:52
  44.5 11.2 %collective-permute-start = (bf16[2,1536]{1,0:T(2,128)(2,1)S(1)}, bf16[2,1536]{1,0:T(2,128)(2,1)S(1)}, u32[]{:S(2)}, u32[]{:S(2)}) collective-permute-start(bf16[2,1536]{1,0:T(2,128)(2,1)S(1)} %get-tuple-element.9), channel_id=1, source_target_pairs={{0,4},{4,8},{8,12},{12,16},{16,20},{20,24},{24,28},{28,32},{32,36}... | collective-permute-start | bytes 18440 | tf_op jit(solution)/shard_map/ppermute | solution.py:18
  47.9 5.5 collective-permute-start.1
  51.5 4.2 copy-start.1
  58.8 76.5 %all-gather.8.cloned.1.call-start = ((), (), s32[]{:S(2)}) async-start(), calls=%async_computation.2 | async-start | bytes 1966080 | tf_op jit(solution)/shard_map/all_gather | solution.py:52
  92.2 8.3 %collective-permute-start.3 = (bf16[4,1536]{1,0:T(4,128)(2,1)S(1)}, bf16[4,1536]{1,0:T(4,128)(2,1)S(1)}, u32[]{:S(2)}, u32[]{:S(2)}) collective-permute-start(bf16[4,1536]{1,0:T(4,128)(2,1)S(1)} %get-tuple-element.8), channel_id=1, source_target_pairs={{4,0},{8,4},{12,8},{16,12},{20,16},{24,20},{28,24},{32,28},{36,32}... | collective-permute-start | bytes 36872 | tf_op jit(solution)/shard_map/ppermute | solution.py:19
  95.8 7.0 copy-start.3
  95.8 7.0 collective-permute-start.2
  105.9 699.5 %all-reduce.2.cloned.1.call-start = ((), (), s32[]{:S(2)}) async-start(), calls=%async_computation.3 | async-start | bytes 1179648 | tf_op jit(solution)/shard_map/psum | solution.py:64
  139.9 8.4 %collective-permute-start.5 = (bf16[8,1536]{1,0:T(8,128)(2,1)S(1)}, bf16[8,1536]{1,0:T(8,128)(2,1)S(1)}, u32[]{:S(2)}, u32[]{:S(2)}) collective-permute-start(bf16[8,1536]{1,0:T(8,128)(2,1)S(1)} %get-tuple-element.6), channel_id=1, source_target_pairs={{4,0},{8,4},{12,8},{16,12},{20,16},{24,20},{28,24},{32,28},{36,32}... | collective-permute-start | bytes 73736 | tf_op jit(solution)/shard_map/ppermute | solution.py:19
  143.7 7.0 copy-start.2
  143.7 7.0 collective-permute-start.4
  150.6 2.4 copy-start.4
  150.6 3.6 copy-start.5
Sparse Core Ops, SparseCore 0:
  10.5 29.3 all-gather.3
  58.9 28.6 all-gather.5
  106.0 29.3 all-gather.7
  154.4 650.8 all-reduce.1
where the time goes:
time: 815 us; the launch traced here: 814 us
  waiting for transfers between devices  740 us (91%)
  matrix products  25.6 us (3%)
  starting transfers between devices  17 us (2%)
  between operations  14.1 us (2%)
  other arithmetic  13.7 us (2%)
    psum x1, waiting for transfers between devices, body(): weight_grad = lax.psum(partial_grad, ('section', 'seq'))  650 us
    all_gather x3, waiting for transfers between devices, body(): full_rows = lax.all_gather(stream, 'chan', axis=1, tiled=True)  87.6 us
  transfers between devices with their start and end apart: 10, of which 5 were waited for; matrix products, arithmetic and copies ran while one was open for 2% of the time, Pallas kernels for 0%

commit v1 on v0

--- a/solution.py
+++ b/solution.py
@@ -6,6 +6,12 @@
 PATCH = 128
 FIRST_DILATION0 = 2
 EPSILON = 1e-06
+
+
+def gather_and_add(block, axis):
+    parts = lax.all_gather(block, axis, axis=0, tiled=False)
+    acc = parts.sum(axis=0)
+    return acc
 
 
 def with_halo(shard, sides, width):
@@ -61,7 +67,7 @@
     partial_grad = lax.dot_general(
         stream, upstream_rows, contract_row_pairs, preferred_element_type=jnp.float32
     )
-    weight_grad = lax.psum(partial_grad, ("section", "seq"))
+    weight_grad = gather_and_add(partial_grad, ("section", "seq"))
     return (decoded[None], weight_grad)
 
 

time: 815 us -> 532 us (0.65)
  waiting for transfers between devices: 740 us -> 443 us
  other arithmetic: 13.7 us -> 27.9 us
    psum x1 -> x0, waiting for transfers between devices: 650 us -> none  [body(): weight_grad = lax.psum(partial_grad, ('section', 'seq'))]
    all_gather x0 -> x1, waiting for transfers between devices: none -> 353 us  [gather_and_add(): parts = lax.all_gather(block, axis, axis=0, tiled=False)]
    reduce_sum x0 -> x1, other arithmetic: none -> 14.1 us  [gather_and_add(): acc = parts.sum(axis=0)]
  transfers between devices with their start and end apart: 10 -> 10, of which waited for: 5 -> 5; matrix products, arithmetic and copies ran while one was open for 2% -> 3% of each run, Pallas kernels for 0% -> 0%
where the time goes in v1:
time: 532 us; the launch traced here: 529 us
  waiting for transfers between devices  443 us (83%)
  other arithmetic  27.9 us (5%)
  matrix products  25.6 us (5%)
  starting transfers between devices  17 us (3%)
  between operations  14.1 us (3%)
    all_gather x1, waiting for transfers between devices, gather_and_add(): parts = lax.all_gather(block, axis, axis=0, tiled=False)  353 us
    all_gather x3, waiting for transfers between devices, body(): full_rows = lax.all_gather(stream, 'chan', axis=1, tiled=True)  87.6 us
    reduce_sum x1, other arithmetic, gather_and_add(): acc = parts.sum(axis=0)  14.1 us
    dot_general x6, matrix products, apply_convolution(): jnp.dot(padded[start:start + row_count], kernel_taps[offset], preferred_e...  13.5 us
    ppermute x3, starting transfers between devices, with_halo(): before = lax.ppermute(last, axis, up)  12.8 us
  transfers between devices with their start and end apart: 10, of which 5 were waited for; matrix products, arithmetic and copies ran while one was open for 3% of the time, Pallas kernels for 0%

profile of v1, /device:TPU:24, one launch (start us, length us, event | category | flops | bytes accessed | tf_op | source)
XLA Modules:
  0.0 529.1 jit_solution(6820795464893698286)
XLA Ops:
  7.2 0.0 copy-start
  7.2 0.0 all-gather.6.cloned.1.call-start
  7.3 0.1 eq.26
  7.4 1.1 copy.8
  8.4 0.2 eq.23
  8.6 0.4 eq.24
  9.0 1.3 convolution_convert_fusion.1
  10.3 0.0 all-gather.6.cloned.1.call-update
  10.4 0.0 all-gather.8.cloned.1.call-start
  10.4 0.1 slice_reduce_fusion
  10.5 29.4 %all-gather.6.cloned.1.call-done = bf16[512,1536]{1,0:T(8,128)(2,1)} async-done(((bf16[512,384]{1,0:T(8,128)(2,1)}), bf16[512,1536]{1,0:T(8,128)(2,1)}) %all-gather.6.cloned.1.call-update) | async-done | bytes 1572880 | tf_op jit(solution)/shard_map/all_gather | solution.py:58
  39.8 1.8 fusion
  41.6 2.8 fusion.4
  44.5 3.5 collective-permute-start
  47.9 1.3 collective-permute-start.1
  49.2 2.2 fusion.60
  51.5 0.0 copy-start.2
  51.5 2.0 collective-permute-done.1
  53.4 2.3 fusion.38
  55.7 3.1 fusion.49
  58.8 0.0 all-gather.8.cloned.1.call-update
  58.8 0.0 all-gather.10.cloned.1.call-start
  58.8 28.8 %all-gather.8.cloned.1.call-done = bf16[512,1536]{1,0:T(8,128)(2,1)} async-done(((bf16[512,384]{1,0:T(8,128)(2,1)}), bf16[512,1536]{1,0:T(8,128)(2,1)}) %all-gather.8.cloned.1.call-update) | async-done | bytes 1572880 | tf_op jit(solution)/shard_map/all_gather | solution.py:58
  87.6 1.8 fusion.9
  89.4 2.8 fusion.13
  92.2 1.3 collective-permute-start.3
  93.5 2.2 fusion.56
  95.8 0.0 copy-start.4
  95.8 4.7 collective-permute-start.2
  100.5 2.3 fusion.34
  102.8 3.1 add_convert_fusion.1
  105.9 0.0 all-gather.10.cloned.1.call-update
  105.9 0.0 all-gather.12.cloned.1.call-start
  105.9 29.4 %all-gather.10.cloned.1.call-done = bf16[512,1536]{1,0:T(8,128)(2,1)} async-done(((bf16[512,384]{1,0:T(8,128)(2,1)}), bf16[512,1536]{1,0:T(8,128)(2,1)}) %all-gather.10.cloned.1.call-update) | async-done | bytes 1572880 | tf_op jit(solution)/shard_map/all_gather | solution.py:58
  135.4 1.8 fusion.18
  137.2 2.8 fusion.22
  140.0 1.5 collective-permute-start.5
  141.4 2.2 fusion.52
  143.7 0.0 copy-start.3
  143.7 4.7 collective-permute-start.4
  148.4 2.2 fusion.30
  150.7 0.0 copy-start.6
  150.7 2.3 add_convert_fusion
  153.1 1.2 fusion.74
  154.3 0.0 all-gather.12.cloned.1.call-update
  154.3 1.1 fusion.50
  155.5 353.0 %all-gather.12.cloned.1.call-done = f32[24576,384]{1,0:T(8,128)} async-done(((f32[384,384]{1,0:T(8,128)}), f32[24576,384]{1,0:T(8,128)}) %all-gather.12.cloned.1.call-update) | async-done | bytes 37748752 | tf_op jit(solution)/shard_map/all_gather | solution.py:12
  508.5 14.1 %reduce_sum.39 = f32[384,384]{1,0:T(8,128)} reduce(f32[64,384,384]{2,1,0:T(8,128)} %bitcast.47, f32[]{:T(128)} %constant.3.clone.1), dimensions={0}, to_apply=%region_3.0 | reduce | flops 9289728 | bytes 38338564 | tf_op jit(solution)/shard_map/reduce_sum | solution.py:13
  (23 shorter events, 0.1 us)
Async XLA Ops:
  7.2 1.8 copy-start
  7.2 3.2 copy-start.7
  7.2 32.7 %all-gather.6.cloned.1.call-start = ((), (), s32[]{:S(2)}) async-start(), calls=%async_computation | async-start | bytes 1966080 | tf_op jit(solution)/shard_map/all_gather | solution.py:58
  10.4 77.3 %all-gather.8.cloned.1.call-start = ((), (), s32[]{:S(2)}) async-start(), calls=%async_computation.1 | async-start | bytes 1966080 | tf_op jit(solution)/shard_map/all_gather | solution.py:58
  44.5 11.2 %collective-permute-start = (bf16[2,1536]{1,0:T(2,128)(2,1)S(1)}, bf16[2,1536]{1,0:T(2,128)(2,1)S(1)}, u32[]{:S(2)}, u32[]{:S(2)}) collective-permute-start(bf16[2,1536]{1,0:T(2,128)(2,1)S(1)} %get-tuple-element.9), channel_id=1, source_target_pairs={{0,4},{4,8},{8,12},{12,16},{16,20},{20,24},{24,28},{28,32},{32,36}... | collective-permute-start | bytes 18440 | tf_op jit(solution)/shard_map/ppermute | solution.py:24
  47.9 5.5 %collective-permute-start.1 = (bf16[2,1536]{1,0:T(2,128)(2,1)S(1)}, bf16[2,1536]{1,0:T(2,128)(2,1)S(1)}, u32[]{:S(2)}, u32[]{:S(2)}) collective-permute-start(bf16[2,1536]{1,0:T(2,128)(2,1)S(1)} %get-tuple-element.10), channel_id=1, source_target_pairs={{4,0},{8,4},{12,8},{16,12},{20,16},{24,20},{28,24},{32,28},{36,32}... | collective-permute-start | bytes 18440 | tf_op jit(solution)/shard_map/ppermute | solution.py:25
  51.5 4.2 copy-start.2
  58.8 76.6 %all-gather.10.cloned.1.call-start = ((), (), s32[]{:S(2)}) async-start(), calls=%async_computation.2 | async-start | bytes 1966080 | tf_op jit(solution)/shard_map/all_gather | solution.py:58
  92.2 8.2 %collective-permute-start.3 = (bf16[4,1536]{1,0:T(4,128)(2,1)S(1)}, bf16[4,1536]{1,0:T(4,128)(2,1)S(1)}, u32[]{:S(2)}, u32[]{:S(2)}) collective-permute-start(bf16[4,1536]{1,0:T(4,128)(2,1)S(1)} %get-tuple-element.8), channel_id=1, source_target_pairs={{4,0},{8,4},{12,8},{16,12},{20,16},{24,20},{28,24},{32,28},{36,32}... | collective-permute-start | bytes 36872 | tf_op jit(solution)/shard_map/ppermute | solution.py:25
  95.8 7.0 %copy-start.4 = (bf16[512,384]{1,0:T(8,128)(2,1)S(1)}, bf16[512,384]{1,0:T(8,128)(2,1)}, u32[]{:S(2)}) copy-start(bf16[512,384]{1,0:T(8,128)(2,1)} %fusion.49) | copy-start | bytes 1179652
  95.8 7.0 %collective-permute-start.2 = (bf16[4,1536]{1,0:T(4,128)(2,1)S(1)}, bf16[4,1536]{1,0:T(4,128)(2,1)S(1)}, u32[]{:S(2)}, u32[]{:S(2)}) collective-permute-start(bf16[4,1536]{1,0:T(4,128)(2,1)S(1)} %get-tuple-element.7), channel_id=1, source_target_pairs={{0,4},{4,8},{8,12},{12,16},{16,20},{20,24},{24,28},{28,32},{32,36}... | collective-permute-start | bytes 36872 | tf_op jit(solution)/shard_map/ppermute | solution.py:24
  105.9 402.6 %all-gather.12.cloned.1.call-start = ((), (), s32[]{:S(2)}) async-start(), calls=%async_computation.3 | async-start | bytes 38338560 | tf_op jit(solution)/shard_map/all_gather | solution.py:12
  140.0 8.4 %collective-permute-start.5 = (bf16[8,1536]{1,0:T(8,128)(2,1)S(1)}, bf16[8,1536]{1,0:T(8,128)(2,1)S(1)}, u32[]{:S(2)}, u32[]{:S(2)}) collective-permute-start(bf16[8,1536]{1,0:T(8,128)(2,1)S(1)} %get-tuple-element.6), channel_id=1, source_target_pairs={{4,0},{8,4},{12,8},{16,12},{20,16},{24,20},{28,24},{32,28},{36,32}... | collective-permute-start | bytes 73736 | tf_op jit(solution)/shard_map/ppermute | solution.py:25
  143.7 7.0 %copy-start.3 = (bf16[512,384]{1,0:T(8,128)(2,1)S(1)}, bf16[512,384]{1,0:T(8,128)(2,1)}, u32[]{:S(2)}) copy-start(bf16[512,384]{1,0:T(8,128)(2,1)} %add_convert_fusion.1) | copy-start | bytes 1179652
  143.7 7.0 %collective-permute-start.4 = (bf16[8,1536]{1,0:T(8,128)(2,1)S(1)}, bf16[8,1536]{1,0:T(8,128)(2,1)S(1)}, u32[]{:S(2)}, u32[]{:S(2)}) collective-permute-start(bf16[8,1536]{1,0:T(8,128)(2,1)S(1)} %get-tuple-element.5), channel_id=1, source_target_pairs={{0,4},{4,8},{8,12},{12,16},{16,20},{20,24},{24,28},{28,32},{32,36}... | collective-permute-start | bytes 73736 | tf_op jit(solution)/shard_map/ppermute | solution.py:24
  150.7 2.4 copy-start.5
  150.7 3.6 copy-start.6
  508.5 14.2 %copy-start.1 = (bf16[512,384]{1,0:T(8,128)(2,1)S(1)}, bf16[512,384]{1,0:T(8,128)(2,1)}, u32[]{:S(2)}) copy-start(bf16[512,384]{1,0:T(8,128)(2,1)} %param.7) | copy-start | bytes 1179652
Sparse Core Ops, SparseCore 0:
  10.5 29.3 all-gather.5
  58.9 28.6 all-gather.7
  106.0 29.3 all-gather.9
  154.4 353.9 all-gather.11
